TPU v7x, 256 devices: a whole 4x4x8 slice. The times are simulated.
256 devices in a mesh: kv: 2 (over core), seq: 128 (over z, y, x).
Axes of the slice: x: 4, y: 4, z: 8, core: 2. Of those that a mesh axis runs over, the one named last changes fastest.
Arguments:
- tokens: bfloat16 [32768, 4096], P(('seq', 'kv')), may hold values from -6 to 6
- gain: float32 [4096], replicated, may hold values from 0.25 to 1.75
- w_query: bfloat16 [4096, 4096], P(None, 'kv'), may hold values from -1 to 1
- w_key: bfloat16 [4096, 1024], P(None, 'kv'), may hold values from -4 to 4
- w_value: bfloat16 [4096, 1024], P(None, 'kv'), may hold values from -0.09375 to 0.09375
- w_out: bfloat16 [4096, 4096], P('kv'), may hold values from -0.09375 to 0.09375
- segment_ids: int32 [32768], replicated, may hold values from 0 to 32767, as said below
- page_table: int32 [256], P('seq'), may hold values from 0 to 1, as said below
Outputs:
- mixed: bfloat16 [32768, 4096], P(('seq', 'kv'))
- attn_out: bfloat16 [32768, 4096], P(('seq', 'kv'))
- page_pool: bfloat16 [256, 2, 8, 128, 128], P('seq', None, 'kv')
Inputs may be any that keep to these rules, and one draw needn't show every extreme that they name: `segment_ids`: never falls along the stream; tokens of one prompt share the position of its first token as id; every prompt has 1 to 2048 tokens; exactly two prompts have 2048 tokens, one in each half of the stream, each beginning inside a block of 256 tokens and not at its first token; every other prompt has fewer than 128 tokens; the last token of the stream is a prompt of its own. `page_table`: in each aligned block of 2 entries every value appears once.
All inputs are finite; a program needn't handle non-finite values.
Results may differ from a plain program's by a relative error of at most 0.0065.
The roundings to bfloat16 on the way count: a program that leaves them out, or rounds other values in their place, can miss the bound.
Values may be sent and summed in bfloat16 or wider, within the bound.
A program may use at most 192 MiB of HBM per device.

v0:
```python
from functools import partial
import jax
import jax.numpy as jnp
from jax import lax
from jax.sharding import PartitionSpec as P

HD = 128
norm_eps = 1e-05


def shifted(value, axis, steps):
    count = lax.axis_size(axis)
    leading, last = (max(0, -steps), min(count, count - steps))
    return lax.ppermute(value, axis, [(source, source + steps) for source in range(leading, last)])


def head_attention(inputs, masks, live, sparse):
    query_head, key_blocks, value_blocks = inputs
    block_count = key_blocks.shape[0]
    key_width = key_blocks.shape[1]
    score_scale = query_head.shape[-1] ** (-0.5)

    def block_scores(distance):
        scores = (
            jnp.einsum(
                "qgd,kd->gqk", query_head, key_blocks[distance], preferred_element_type=jnp.float32
            )
            * score_scale
        )
        return jnp.where(masks[distance][None], scores, -jnp.inf)

    pieces = [block_scores(0)]
    for distance in range(1, block_count):
        pieces.append(block_scores(distance))
    scores = jnp.concatenate(pieces, axis=2)
    row_peak = jnp.max(scores, axis=2, keepdims=True)
    weights = jnp.exp(scores - row_peak).astype(jnp.bfloat16)
    row_total = jnp.sum(weights, axis=2, dtype=jnp.float32)
    all_values = value_blocks.reshape(block_count * key_width, value_blocks.shape[-1])
    weighted = jnp.einsum("gqk,kd->qgd", weights, all_values, preferred_element_type=jnp.float32)
    return (weighted / row_total.T[:, :, None]).astype(jnp.bfloat16)


def shards(tokens, gain, w_query, w_key, w_value, w_out, segment_ids, page_table):
    tok_rows = tokens.shape[0]
    block_rows = tok_rows * lax.axis_size("kv")
    reach = min(8, lax.axis_size("seq") // 2 - 1)
    kv_local = w_key.shape[1] // HD
    q_local = w_query.shape[1] // HD
    group_size = q_local // kv_local
    wide_rows = tokens.astype(jnp.float32)
    normed = (
        wide_rows
        * lax.rsqrt(jnp.mean(wide_rows * wide_rows, axis=1, keepdims=True) + norm_eps)
        * gain
    ).astype(jnp.bfloat16)
    piece = lax.all_gather(normed, "kv", axis=0, tiled=True)
    projected = jnp.concatenate(
        [
            jnp.dot(piece, w_query, preferred_element_type=jnp.float32),
            jnp.dot(piece, w_key, preferred_element_type=jnp.float32),
            jnp.dot(piece, w_value, preferred_element_type=jnp.float32),
        ],
        axis=1,
    ).astype(jnp.bfloat16)
    query_cols = q_local * HD
    key_cols = kv_local * HD
    query = projected[:, :query_cols].reshape(block_rows, kv_local, group_size, HD)
    key_rows = projected[:, query_cols : query_cols + key_cols].reshape(block_rows, kv_local, HD)
    value_rows = projected[:, query_cols + key_cols :].reshape(block_rows, kv_local, HD)
    pair_rows = jnp.stack([key_rows, value_rows], axis=0)
    page_rows = page_table.shape[0]
    page_len = block_rows // page_rows
    pages = pair_rows.reshape(2, page_rows, page_len, kv_local, HD).transpose(1, 0, 3, 2, 4)
    page_pool = jnp.zeros_like(pages).at[page_table].set(pages)
    received = [pair_rows]
    carried = pair_rows
    for distance in range(1, reach + 1):
        carried = shifted(carried, "seq", 1)
        received.append(carried)
    stacked_pairs = jnp.stack(received, axis=1)
    seq_index = lax.axis_index("seq")
    query_segs = lax.dynamic_slice_in_dim(segment_ids, seq_index * block_rows, block_rows)
    lower = jnp.arange(block_rows)[None, :] <= jnp.arange(block_rows)[:, None]
    mask_list = []
    live_list = []
    for distance in range(reach + 1):
        source = jnp.maximum(seq_index - distance, 0)
        valid = seq_index - distance >= 0
        key_segs = lax.dynamic_slice_in_dim(segment_ids, source * block_rows, block_rows)
        same = (key_segs[None, :] == query_segs[:, None]) & valid
        if distance == 0:
            same = same & lower
            live_list.append(jnp.array(True))
        else:
            live_list.append(valid & (key_segs[block_rows - 1] == query_segs[0]))
        mask_list.append(same)
    masks = jnp.stack(mask_list)
    live = jnp.stack(live_list)
    heads_out = lax.map(
        partial(head_attention, masks=masks, live=live, sparse=False),
        (
            query.transpose(1, 0, 2, 3),
            stacked_pairs[0].transpose(2, 0, 1, 3),
            stacked_pairs[1].transpose(2, 0, 1, 3),
        ),
    )
    attention = heads_out.transpose(1, 0, 2, 3).reshape(block_rows, q_local * HD)
    summed = lax.psum(jnp.dot(attention, w_out, preferred_element_type=jnp.float32), "kv")
    branch = lax.dynamic_slice_in_dim(summed, lax.axis_index("kv") * tok_rows, tok_rows, 0)
    attn_out = branch.astype(jnp.bfloat16)
    mixed = (wide_rows + branch).astype(jnp.bfloat16)
    return (mixed, attn_out, page_pool)


def solution(mesh):
    in_specs = (
        P(("seq", "kv"), None),
        P(),
        P(None, "kv"),
        P(None, "kv"),
        P(None, "kv"),
        P("kv", None),
        P(),
        P("seq"),
    )
    out_specs = (P(("seq", "kv"), None), P(("seq", "kv"), None), P("seq", None, "kv", None, None))
    return jax.shard_map(shards, mesh=mesh, in_specs=in_specs, out_specs=out_specs, check_vma=False)
```

profile of v0, /device:TPU:1, one launch (start us, length us, event | category | flops | bytes accessed | tf_op | source)
XLA Modules:
  0.0 373.4 jit_solution(7717644761476916831)
XLA Ops:
  8.7 2.5 fusion.73
  11.3 20.5 %all-gather.2.cloned.1.call-done = bf16[256,4096]{1,0:T(8,128)(2,1)} async-done(((bf16[128,4096]{1,0:T(8,128)(2,1)}), bf16[256,4096]{1,0:T(8,128)(2,1)}) %all-gather.2.cloned.1.call-update) | async-done | bytes 2097168 | tf_op jit(solution)/shard_map/all_gather | solution.py:57
  31.9 4.1 %convolution_convert_fusion.2 = bf16[256,512]{1,0:T(8,128)(2,1)S(1)} fusion(bf16[256,4096]{1,0:T(8,128)(2,1)} %all-gather.2.cloned.1.call-done, bf16[4096,512]{1,0:T(8,128)(2,1)} %param.13), kind=kOutput, calls=%fused_computation.115 | convolution fusion | flops 1073872896 | bytes 6553600 | tf_op jit(solution)/shard_map/dot_general | solution.py:61
  36.1 4.1 %convolution_convert_fusion.1 = bf16[256,512]{1,0:T(8,128)(2,1)S(1)} fusion(bf16[256,4096]{1,0:T(8,128)(2,1)} %all-gather.2.cloned.1.call-done, bf16[4096,512]{1,0:T(8,128)(2,1)} %param.14), kind=kOutput, calls=%fused_computation.114 | convolution fusion | flops 1073872896 | bytes 6553600 | tf_op jit(solution)/shard_map/dot_general | solution.py:62
  40.3 2.9 collective-permute-start
  43.1 11.0 %collective-permute-done = bf16[2,256,4,128]{3,1,2,0:T(8,128)(2,1)S(1)} collective-permute-done((bf16[2,256,4,128]{3,1,2,0:T(8,128)(2,1)S(1)}, bf16[2,256,4,128]{3,1,2,0:T(8,128)(2,1)S(1)}, u32[]{:S(2)}, u32[]{:S(2)}) %collective-permute-start) | collective-permute-done | bytes 524320 | tf_op jit(solution)/shard_map/ppermute | solution.py:14
  54.1 4.1 %collective-permute-start.1 = (bf16[2,256,4,128]{3,1,2,0:T(8,128)(2,1)S(1)}, bf16[2,256,4,128]{3,1,2,0:T(8,128)(2,1)S(1)}, u32[]{:S(2)}, u32[]{:S(2)}) collective-permute-start(bf16[2,256,4,128]{3,1,2,0:T(8,128)(2,1)S(1)} %collective-permute-done), channel_id=1, source_target_pairs={{0,1},{1,2},{2,3},{3,4},{4,5},{5,6},{6,7},{7,8},{8,9},{9,10},{10,1... | collective-permute-start | bytes 1572872 | tf_op jit(solution)/shard_map/ppermute | solution.py:14
  58.3 10.2 %collective-permute-done.1 = bf16[2,256,4,128]{3,1,2,0:T(8,128)(2,1)S(1)} collective-permute-done((bf16[2,256,4,128]{3,1,2,0:T(8,128)(2,1)S(1)}, bf16[2,256,4,128]{3,1,2,0:T(8,128)(2,1)S(1)}, u32[]{:S(2)}, u32[]{:S(2)}) %collective-permute-start.1) | collective-permute-done | bytes 524320 | tf_op jit(solution)/shard_map/ppermute | solution.py:14
  68.4 4.1 %collective-permute-start.2 = (bf16[2,256,4,128]{3,1,2,0:T(8,128)(2,1)S(1)}, bf16[2,256,4,128]{3,1,2,0:T(8,128)(2,1)S(1)}, u32[]{:S(2)}, u32[]{:S(2)}) collective-permute-start(bf16[2,256,4,128]{3,1,2,0:T(8,128)(2,1)S(1)} %collective-permute-done.1), channel_id=1, source_target_pairs={{0,1},{1,2},{2,3},{3,4},{4,5},{5,6},{6,7},{7,8},{8,9},{9,10},{10,1... | collective-permute-start | bytes 1572872 | tf_op jit(solution)/shard_map/ppermute | solution.py:14
  72.6 9.3 %collective-permute-done.2 = bf16[2,256,4,128]{3,1,2,0:T(8,128)(2,1)S(1)} collective-permute-done((bf16[2,256,4,128]{3,1,2,0:T(8,128)(2,1)S(1)}, bf16[2,256,4,128]{3,1,2,0:T(8,128)(2,1)S(1)}, u32[]{:S(2)}, u32[]{:S(2)}) %collective-permute-start.2) | collective-permute-done | bytes 524320 | tf_op jit(solution)/shard_map/ppermute | solution.py:14
  82.7 4.1 %collective-permute-start.3 = (bf16[2,256,4,128]{3,1,2,0:T(8,128)(2,1)S(1)}, bf16[2,256,4,128]{3,1,2,0:T(8,128)(2,1)S(1)}, u32[]{:S(2)}, u32[]{:S(2)}) collective-permute-start(bf16[2,256,4,128]{3,1,2,0:T(8,128)(2,1)S(1)} %collective-permute-done.2), channel_id=1, source_target_pairs={{0,1},{1,2},{2,3},{3,4},{4,5},{5,6},{6,7},{7,8},{8,9},{9,10},{10,1... | collective-permute-start | bytes 1572872 | tf_op jit(solution)/shard_map/ppermute | solution.py:14
  86.8 8.4 %collective-permute-done.3 = bf16[2,256,4,128]{3,1,2,0:T(8,128)(2,1)S(1)} collective-permute-done((bf16[2,256,4,128]{3,1,2,0:T(8,128)(2,1)S(1)}, bf16[2,256,4,128]{3,1,2,0:T(8,128)(2,1)S(1)}, u32[]{:S(2)}, u32[]{:S(2)}) %collective-permute-start.3) | collective-permute-done | bytes 524320 | tf_op jit(solution)/shard_map/ppermute | solution.py:14
  95.2 4.9 %collective-permute-start.4 = (bf16[2,256,4,128]{3,1,2,0:T(8,128)(2,1)S(1)}, bf16[2,256,4,128]{3,1,2,0:T(8,128)(2,1)}, u32[]{:S(2)}, u32[]{:S(2)}) collective-permute-start(bf16[2,256,4,128]{3,1,2,0:T(8,128)(2,1)S(1)} %collective-permute-done.3), channel_id=1, source_target_pairs={{0,1},{1,2},{2,3},{3,4},{4,5},{5,6},{6,7},{7,8},{8,9},{9,10},{10,1... | collective-permute-start | bytes 1572872 | tf_op jit(solution)/shard_map/ppermute | solution.py:14
  101.3 5.7 %collective-permute-done.4 = bf16[2,256,4,128]{3,1,2,0:T(8,128)(2,1)} collective-permute-done((bf16[2,256,4,128]{3,1,2,0:T(8,128)(2,1)S(1)}, bf16[2,256,4,128]{3,1,2,0:T(8,128)(2,1)}, u32[]{:S(2)}, u32[]{:S(2)}) %collective-permute-start.4) | collective-permute-done | bytes 524320 | tf_op jit(solution)/shard_map/ppermute | solution.py:14
  107.0 5.8 %collective-permute-start.5 = (bf16[2,256,4,128]{3,1,2,0:T(8,128)(2,1)}, bf16[2,256,4,128]{3,1,2,0:T(8,128)(2,1)}, u32[]{:S(2)}, u32[]{:S(2)}) collective-permute-start(bf16[2,256,4,128]{3,1,2,0:T(8,128)(2,1)} %collective-permute-done.4), channel_id=1, source_target_pairs={{0,1},{1,2},{2,3},{3,4},{4,5},{5,6},{6,7},{7,8},{8,9},{9,10},{10,1... | collective-permute-start | bytes 1572872 | tf_op jit(solution)/shard_map/ppermute | solution.py:14
  112.8 10.9 %convolution_convert_fusion = bf16[256,2048]{1,0:T(8,128)(2,1)S(1)} fusion(bf16[256,4096]{1,0:T(8,128)(2,1)} %all-gather.2.cloned.1.call-done, bf16[4096,2048]{1,0:T(8,128)(2,1)} %param.12), kind=kOutput, calls=%fused_computation.106 | convolution fusion | flops 4295491584 | bytes 19922944 | tf_op jit(solution)/shard_map/dot_general | solution.py:60
  126.9 5.5 %collective-permute-start.6 = (bf16[2,256,4,128]{3,1,2,0:T(8,128)(2,1)}, bf16[2,256,4,128]{3,1,2,0:T(8,128)(2,1)S(1)}, u32[]{:S(2)}, u32[]{:S(2)}) collective-permute-start(bf16[2,256,4,128]{3,1,2,0:T(8,128)(2,1)} %collective-permute-done.5), channel_id=1, source_target_pairs={{0,1},{1,2},{2,3},{3,4},{4,5},{5,6},{6,7},{7,8},{8,9},{9,10},{10,1... | collective-permute-start | bytes 1572872 | tf_op jit(solution)/shard_map/ppermute | solution.py:14
  133.6 5.5 %collective-permute-done.6 = bf16[2,256,4,128]{3,1,2,0:T(8,128)(2,1)S(1)} collective-permute-done((bf16[2,256,4,128]{3,1,2,0:T(8,128)(2,1)}, bf16[2,256,4,128]{3,1,2,0:T(8,128)(2,1)S(1)}, u32[]{:S(2)}, u32[]{:S(2)}) %collective-permute-start.6) | collective-permute-done | bytes 524320 | tf_op jit(solution)/shard_map/ppermute | solution.py:14
  139.1 6.4 %collective-permute-start.7 = (bf16[2,256,4,128]{3,1,2,0:T(8,128)(2,1)S(1)}, bf16[2,256,4,128]{3,1,2,0:T(8,128)(2,1)S(1)}, u32[]{:S(2)}, u32[]{:S(2)}) collective-permute-start(bf16[2,256,4,128]{3,1,2,0:T(8,128)(2,1)S(1)} %collective-permute-done.6), channel_id=1, source_target_pairs={{0,1},{1,2},{2,3},{3,4},{4,5},{5,6},{6,7},{7,8},{8,9},{9,10},{10,1... | collective-permute-start | bytes 1572872 | tf_op jit(solution)/shard_map/ppermute | solution.py:14
  147.8 3.6 collective-permute-done.7
  153.2 120.6 %while.12 = (s32[]{:T(128)}, bf16[4,256,4,128]{1,3,2,0:T(8,128)(2,1)}, bf16[4,9,256,128]{3,2,1,0:T(8,128)(2,1)S(1)}, bf16[4,9,256,128]{3,2,1,0:T(8,128)(2,1)}, b...) while((s32[]{:T(128)}, ...), condition=%wide.region_12.13_spmd.clone.clone, body=%wide.region_1.12_spmd.clone.clone.sunk | while | flops 1230764032 | bytes 72335304 | solution.py:100
  153.8 2.3 fusion.107
  156.1 2.3 fusion.108
  160.7 2.3 fusion.110
  163.0 2.4 fusion.111
  165.3 2.3 fusion.112
  167.6 2.3 fusion.113
  169.9 2.3 fusion.114
  172.2 2.3 fusion.115
  174.6 5.1 %convert_reduce_fusion.2 = f32[4,256]{1,0:T(4,128)S(1)} fusion(f32[4,256,2304]{1,2,0:T(8,128)} %get-tuple-element.530, f32[4,256]{1,0:T(4,128)S(1)} %maximum_maximum_fusion.2), kind=kLoop, calls=%fused_computation.10.clone.1 | loop fusion | flops 9436160 | bytes 9445376 | tf_op jit(solution)/shard_map/while/body/eval_jaxpr/reduce_sum | solution.py:38
  180.9 2.4 fusion.116
  184.0 2.3 fusion.107
  186.3 2.3 fusion.108
  190.8 2.3 fusion.110
  193.1 2.4 fusion.111
  195.5 2.3 fusion.112
  197.8 2.3 fusion.113
  200.1 2.3 fusion.114
  202.4 2.3 fusion.115
  204.7 5.1 %convert_reduce_fusion.2 = f32[4,256]{1,0:T(4,128)S(1)} fusion(f32[4,256,2304]{1,2,0:T(8,128)} %get-tuple-element.530, f32[4,256]{1,0:T(4,128)S(1)} %maximum_maximum_fusion.2), kind=kLoop, calls=%fused_computation.10.clone.1 | loop fusion | flops 9436160 | bytes 9445376 | tf_op jit(solution)/shard_map/while/body/eval_jaxpr/reduce_sum | solution.py:38
  211.1 2.4 fusion.116
  214.1 2.3 fusion.107
  216.4 2.3 fusion.108
  221.0 2.3 fusion.110
  223.3 2.4 fusion.111
  225.6 2.3 fusion.112
  227.9 2.3 fusion.113
  230.2 2.3 fusion.114
  232.5 2.3 fusion.115
  234.9 5.1 %convert_reduce_fusion.2 = f32[4,256]{1,0:T(4,128)S(1)} fusion(f32[4,256,2304]{1,2,0:T(8,128)} %get-tuple-element.530, f32[4,256]{1,0:T(4,128)S(1)} %maximum_maximum_fusion.2), kind=kLoop, calls=%fused_computation.10.clone.1 | loop fusion | flops 9436160 | bytes 9445376 | tf_op jit(solution)/shard_map/while/body/eval_jaxpr/reduce_sum | solution.py:38
  241.2 2.4 fusion.116
  244.3 2.3 fusion.107
  251.1 2.3 fusion.110
  253.4 2.4 fusion.111
  255.8 2.3 fusion.112
  258.1 2.3 fusion.113
  260.4 2.3 fusion.114
  262.7 2.3 fusion.115
  265.0 5.1 %convert_reduce_fusion.2 = f32[4,256]{1,0:T(4,128)S(1)} fusion(f32[4,256,2304]{1,2,0:T(8,128)} %get-tuple-element.530, f32[4,256]{1,0:T(4,128)S(1)} %maximum_maximum_fusion.2), kind=kLoop, calls=%fused_computation.10.clone.1 | loop fusion | flops 9436160 | bytes 9445376 | tf_op jit(solution)/shard_map/while/body/eval_jaxpr/reduce_sum | solution.py:38
  271.4 2.4 fusion.116
  273.8 12.7 %fusion.85 = f32[256,4096]{1,0:T(8,128)} fusion(bf16[256,2048]{0,1:T(8,128)(2,1)} %bitcast.280, bf16[2048,4096]{1,0:T(8,128)(2,1)} %param.15), kind=kOutput, calls=%fused_computation.141 | convolution fusion | flops 4294967296 | bytes 22020096 | tf_op jit(solution)/shard_map/dot_general | solution.py:109
  287.7 73.3 %all-reduce.2.cloned.1.call-done = f32[256,4096]{1,0:T(8,128)} async-done(((f32[256,4096]{1,0:T(8,128)}), f32[256,4096]{1,0:T(8,128)}) %all-reduce.2.cloned.1.call-update) | async-done | bytes 4194320 | tf_op jit(solution)/shard_map/psum | solution.py:109
  361.1 2.7 dynamic-slice_convert_fusion
  363.7 2.8 fusion.74
  (76 shorter events, 32.4 us)
Async XLA Ops:
  7.2 24.7 %all-gather.2.cloned.1.call-start = ((), (), s32[]{:S(2)}) async-start(), calls=%async_computation | async-start | bytes 3145728 | tf_op jit(solution)/shard_map/all_gather | solution.py:57
  11.3 349.8 %all-reduce.2.cloned.1.call-start = ((), (), s32[]{:S(2)}) async-start(), calls=%async_computation.1 | async-start | bytes 8388608 | tf_op jit(solution)/shard_map/psum | solution.py:109
  40.3 13.9 %collective-permute-start = (bf16[2,256,4,128]{3,1,2,0:T(8,128)(2,1)S(1)}, bf16[2,256,4,128]{3,1,2,0:T(8,128)(2,1)S(1)}, u32[]{:S(2)}, u32[]{:S(2)}) collective-permute-start(bf16[2,256,4,128]{3,1,2,0:T(8,128)(2,1)S(1)} %copy_dynamic-update-slice_fusion), channel_id=1, source_target_pairs={{0,1},{1,2},{2,3},{3,4},{4,5},{5,6},{6,7},{7,8},{8,9},{9,10},{10,1... | collective-permute-start | bytes 1572872 | tf_op jit(solution)/shard_map/ppermute | solution.py:14
  54.1 52.8 %copy-start.4 = (bf16[2,256,4,128]{3,1,2,0:T(8,128)(2,1)}, bf16[2,256,4,128]{3,1,2,0:T(8,128)(2,1)S(1)}, u32[]{:S(2)}) copy-start(bf16[2,256,4,128]{3,1,2,0:T(8,128)(2,1)S(1)} %collective-permute-done) | copy-start | bytes 1572868
  54.1 14.3 %collective-permute-start.1 = (bf16[2,256,4,128]{3,1,2,0:T(8,128)(2,1)S(1)}, bf16[2,256,4,128]{3,1,2,0:T(8,128)(2,1)S(1)}, u32[]{:S(2)}, u32[]{:S(2)}) collective-permute-start(bf16[2,256,4,128]{3,1,2,0:T(8,128)(2,1)S(1)} %collective-permute-done), channel_id=1, source_target_pairs={{0,1},{1,2},{2,3},{3,4},{4,5},{5,6},{6,7},{7,8},{8,9},{9,10},{10,1... | collective-permute-start | bytes 1572872 | tf_op jit(solution)/shard_map/ppermute | solution.py:14
  68.4 38.5 %copy-start.3 = (bf16[2,256,4,128]{3,1,2,0:T(8,128)(2,1)}, bf16[2,256,4,128]{3,1,2,0:T(8,128)(2,1)S(1)}, u32[]{:S(2)}) copy-start(bf16[2,256,4,128]{3,1,2,0:T(8,128)(2,1)S(1)} %collective-permute-done.1) | copy-start | bytes 1572868
  68.4 13.4 %collective-permute-start.2 = (bf16[2,256,4,128]{3,1,2,0:T(8,128)(2,1)S(1)}, bf16[2,256,4,128]{3,1,2,0:T(8,128)(2,1)S(1)}, u32[]{:S(2)}, u32[]{:S(2)}) collective-permute-start(bf16[2,256,4,128]{3,1,2,0:T(8,128)(2,1)S(1)} %collective-permute-done.1), channel_id=1, source_target_pairs={{0,1},{1,2},{2,3},{3,4},{4,5},{5,6},{6,7},{7,8},{8,9},{9,10},{10,1... | collective-permute-start | bytes 1572872 | tf_op jit(solution)/shard_map/ppermute | solution.py:14
  81.9 0.8 copy-start.5
  82.7 12.6 %collective-permute-start.3 = (bf16[2,256,4,128]{3,1,2,0:T(8,128)(2,1)S(1)}, bf16[2,256,4,128]{3,1,2,0:T(8,128)(2,1)S(1)}, u32[]{:S(2)}, u32[]{:S(2)}) collective-permute-start(bf16[2,256,4,128]{3,1,2,0:T(8,128)(2,1)S(1)} %collective-permute-done.2), channel_id=1, source_target_pairs={{0,1},{1,2},{2,3},{3,4},{4,5},{5,6},{6,7},{7,8},{8,9},{9,10},{10,1... | collective-permute-start | bytes 1572872 | tf_op jit(solution)/shard_map/ppermute | solution.py:14
  95.2 17.5 %copy-start.7 = (bf16[2,256,4,128]{3,1,2,0:T(8,128)(2,1)}, bf16[2,256,4,128]{3,1,2,0:T(8,128)(2,1)S(1)}, u32[]{:S(2)}) copy-start(bf16[2,256,4,128]{3,1,2,0:T(8,128)(2,1)S(1)} %collective-permute-done.3) | copy-start | bytes 1572868
  95.2 11.7 %collective-permute-start.4 = (bf16[2,256,4,128]{3,1,2,0:T(8,128)(2,1)S(1)}, bf16[2,256,4,128]{3,1,2,0:T(8,128)(2,1)}, u32[]{:S(2)}, u32[]{:S(2)}) collective-permute-start(bf16[2,256,4,128]{3,1,2,0:T(8,128)(2,1)S(1)} %collective-permute-done.3), channel_id=1, source_target_pairs={{0,1},{1,2},{2,3},{3,4},{4,5},{5,6},{6,7},{7,8},{8,9},{9,10},{10,1... | collective-permute-start | bytes 1572872 | tf_op jit(solution)/shard_map/ppermute | solution.py:14
  107.0 19.9 %collective-permute-start.5 = (bf16[2,256,4,128]{3,1,2,0:T(8,128)(2,1)}, bf16[2,256,4,128]{3,1,2,0:T(8,128)(2,1)}, u32[]{:S(2)}, u32[]{:S(2)}) collective-permute-start(bf16[2,256,4,128]{3,1,2,0:T(8,128)(2,1)} %collective-permute-done.4), channel_id=1, source_target_pairs={{0,1},{1,2},{2,3},{3,4},{4,5},{5,6},{6,7},{7,8},{8,9},{9,10},{10,1... | collective-permute-start | bytes 1572872 | tf_op jit(solution)/shard_map/ppermute | solution.py:14
  124.4 9.0 %copy-start.6 = (bf16[2,256,4,128]{3,1,2,0:T(8,128)(2,1)S(1)}, bf16[2,256,4,128]{3,1,2,0:T(8,128)(2,1)}, u32[]{:S(2)}) copy-start(bf16[2,256,4,128]{3,1,2,0:T(8,128)(2,1)} %copy-done.5) | copy-start | bytes 1572868
  124.4 9.1 %copy-start.8 = (bf16[2,256,4,128]{3,1,2,0:T(8,128)(2,1)S(1)}, bf16[2,256,4,128]{3,1,2,0:T(8,128)(2,1)}, u32[]{:S(2)}) copy-start(bf16[2,256,4,128]{3,1,2,0:T(8,128)(2,1)} %copy-done.7) | copy-start | bytes 1572868
  126.9 12.2 %collective-permute-start.6 = (bf16[2,256,4,128]{3,1,2,0:T(8,128)(2,1)}, bf16[2,256,4,128]{3,1,2,0:T(8,128)(2,1)S(1)}, u32[]{:S(2)}, u32[]{:S(2)}) collective-permute-start(bf16[2,256,4,128]{3,1,2,0:T(8,128)(2,1)} %collective-permute-done.5), channel_id=1, source_target_pairs={{0,1},{1,2},{2,3},{3,4},{4,5},{5,6},{6,7},{7,8},{8,9},{9,10},{10,1... | collective-permute-start | bytes 1572872 | tf_op jit(solution)/shard_map/ppermute | solution.py:14
  139.1 12.3 %collective-permute-start.7 = (bf16[2,256,4,128]{3,1,2,0:T(8,128)(2,1)S(1)}, bf16[2,256,4,128]{3,1,2,0:T(8,128)(2,1)S(1)}, u32[]{:S(2)}, u32[]{:S(2)}) collective-permute-start(bf16[2,256,4,128]{3,1,2,0:T(8,128)(2,1)S(1)} %collective-permute-done.6), channel_id=1, source_target_pairs={{0,1},{1,2},{2,3},{3,4},{4,5},{5,6},{6,7},{7,8},{8,9},{9,10},{10,1... | collective-permute-start | bytes 1572872 | tf_op jit(solution)/shard_map/ppermute | solution.py:14
  174.6 6.4 %copy-start = (f32[4,256,2304]{1,2,0:T(8,128)S(1)}, f32[4,256,2304]{1,2,0:T(8,128)}, u32[]{:S(2)}) copy-start(f32[4,256,2304]{1,2,0:T(8,128)} %get-tuple-element.530) | copy-start | bytes 28311556 | tf_op jit(solution)/shard_map/while
  204.7 6.4 %copy-start = (f32[4,256,2304]{1,2,0:T(8,128)S(1)}, f32[4,256,2304]{1,2,0:T(8,128)}, u32[]{:S(2)}) copy-start(f32[4,256,2304]{1,2,0:T(8,128)} %get-tuple-element.530) | copy-start | bytes 28311556 | tf_op jit(solution)/shard_map/while
  234.9 6.4 %copy-start = (f32[4,256,2304]{1,2,0:T(8,128)S(1)}, f32[4,256,2304]{1,2,0:T(8,128)}, u32[]{:S(2)}) copy-start(f32[4,256,2304]{1,2,0:T(8,128)} %get-tuple-element.530) | copy-start | bytes 28311556 | tf_op jit(solution)/shard_map/while
  265.0 6.4 %copy-start = (f32[4,256,2304]{1,2,0:T(8,128)S(1)}, f32[4,256,2304]{1,2,0:T(8,128)}, u32[]{:S(2)}) copy-start(f32[4,256,2304]{1,2,0:T(8,128)} %get-tuple-element.530) | copy-start | bytes 28311556 | tf_op jit(solution)/shard_map/while
  273.8 12.7 %copy-start.9 = (s32[2]{0:T(128)S(1)}, s32[2]{0:T(128)}, u32[]{:S(2)}) copy-start(s32[2]{0:T(128)} %param.17) | copy-start | bytes 28
  286.5 77.2 %copy-start.1 = (bf16[128,4096]{1,0:T(8,128)(2,1)S(1)}, bf16[128,4096]{1,0:T(8,128)(2,1)}, u32[]{:S(2)}) copy-start(bf16[128,4096]{1,0:T(8,128)(2,1)} %param.10) | copy-start | bytes 3145732
  287.7 78.8 %copy-start.2 = (bf16[2,2,4,128,128]{4,3,2,1,0:T(8,128)(2,1)}, bf16[2,2,4,128,128]{4,3,2,1,0:T(8,128)(2,1)S(1)}, u32[]{:S(2)}) copy-start(bf16[2,2,4,128,128]{4,3,2,1,0:T(8,128)(2,1)S(1)} %scatter_fusion) | copy-start | bytes 1572868
Sparse Core Ops, SparseCore 0:
  11.4 20.4 all-gather.1
  286.6 74.3 all-reduce.1
where the time goes:
time: 375 us; the launch traced here: 373 us
  waiting for transfers between devices  148 us (39%)
  matrix products  124 us (33%)
  starting transfers between devices  37.9 us (10%)
  other arithmetic  29.6 us (8%)
  local copies, waits for them, and re-layouts  19.6 us (5%)
  between operations  14.3 us (4%)
    dot_general x36, matrix products, block_scores(): jnp.einsum('qgd,kd->gqk', query_head, key_blocks[distance], preferred_ele...  82.9 us
    psum x1, waiting for transfers between devices, shards(): lax.psum(jnp.dot(attention, w_out, preferred_element_type=jnp.float32), '...  73.3 us
    ppermute x8, waiting for transfers between devices, shifted(): lax.ppermute(value, axis, [(source, source + steps) for source in range(l...  53.6 us
    ppermute x8, starting transfers between devices, shifted(): lax.ppermute(value, axis, [(source, source + steps) for source in range(l...  37.8 us
    all_gather x1, waiting for transfers between devices, shards(): piece = lax.all_gather(normed, 'kv', axis=0, tiled=True)  20.5 us
    reduce_sum x4, other arithmetic, head_attention(): row_total = jnp.sum(weights, axis=2, dtype=jnp.float32)  20.3 us
    dot_general x1, matrix products, shards(): jnp.dot(attention, w_out, preferred_element_type=jnp.float32)  12.7 us
    dot_general x1, matrix products, shards(): jnp.dot(piece, w_query, preferred_element_type=jnp.float32)  10.9 us
  transfers between devices with their start and end apart: 10, of which 9 were waited for; matrix products, arithmetic and copies ran while one was open for 5% of the time, Pallas kernels for 0%

commit v1 on v0

--- a/solution.py
+++ b/solution.py
@@ -54,7 +54,9 @@
         * lax.rsqrt(jnp.mean(wide_rows * wide_rows, axis=1, keepdims=True) + norm_eps)
         * gain
     ).astype(jnp.bfloat16)
-    piece = lax.all_gather(normed, "kv", axis=0, tiled=True)
+    piece = jnp.concatenate(
+        lax.all_to_all(jnp.stack([normed] * lax.axis_size("kv")), "kv", 0, 0), axis=0
+    )
     projected = jnp.concatenate(
         [
             jnp.dot(piece, w_query, preferred_element_type=jnp.float32),

time: 375 us -> 358 us (0.955)
  waiting for transfers between devices: 148 us -> 128 us
  blocking collectives: 0 us -> 8.25 us
  matrix products: 124 us -> 119 us
    all_gather x1 -> x0, waiting for transfers between devices: 20.5 us -> none  [shards(): piece = lax.all_gather(normed, 'kv', axis=0, tiled=True)]
    all_to_all x0 -> x1, blocking collectives: none -> 8.25 us  [shards(): lax.all_to_all(jnp.stack([normed] * lax.axis_size('kv')), 'kv', 0, 0)]
    psum x1, waiting for transfers between devices: 73.3 us -> 79.6 us  [shards(): lax.psum(jnp.dot(attention, w_out, preferred_element_type=jnp.float32), '...]
    ppermute x8, waiting for transfers between devices: 53.6 us -> 48.8 us  [shifted(): lax.ppermute(value, axis, [(source, source + steps) for source in range(l...]
  transfers between devices with their start and end apart: 10 -> 9, of which waited for: 9 -> 8; matrix products, arithmetic and copies ran while one was open for 5% -> 5% of each run, Pallas kernels for 0% -> 0%
where the time goes in v1:
time: 358 us; the launch traced here: 357 us
  waiting for transfers between devices  128 us (36%)
  matrix products  119 us (33%)
  starting transfers between devices  37.5 us (10%)
  other arithmetic  28.9 us (8%)
  local copies, waits for them, and re-layouts  19.8 us (6%)
  between operations  14.4 us (4%)
  blocking collectives  8.25 us (2%)
    dot_general x36, matrix products, block_scores(): jnp.einsum('qgd,kd->gqk', query_head, key_blocks[distance], preferred_ele...  82.9 us
    psum x1, waiting for transfers between devices, shards(): lax.psum(jnp.dot(attention, w_out, preferred_element_type=jnp.float32), '...  79.6 us
    ppermute x8, waiting for transfers between devices, shifted(): lax.ppermute(value, axis, [(source, source + steps) for source in range(l...  48.8 us
    ppermute x8, starting transfers between devices, shifted(): lax.ppermute(value, axis, [(source, source + steps) for source in range(l...  37.5 us
    reduce_sum x4, other arithmetic, head_attention(): row_total = jnp.sum(weights, axis=2, dtype=jnp.float32)  20.3 us
    dot_general x1, matrix products, shards(): jnp.dot(attention, w_out, preferred_element_type=jnp.float32)  12.7 us
    dot_general x4, matrix products, head_attention(): jnp.einsum('gqk,kd->qgd', weights, all_values, preferred_element_type=jnp...  9.76 us
    dot_general x1, matrix products, shards(): jnp.dot(piece, w_query, preferred_element_type=jnp.float32)  9.21 us
  transfers between devices with their start and end apart: 9, of which 8 were waited for; matrix products, arithmetic and copies ran while one was open for 5% of the time, Pallas kernels for 0%

profile of v1, /device:TPU:1, one launch (start us, length us, event | category | flops | bytes accessed | tf_op | source)
XLA Modules:
  0.0 356.6 jit_solution(2982015184780136370)
XLA Ops:
  10.6 8.2 %all_to_all.5 = bf16[2,128,4096]{2,1,0:T(8,128)(2,1)S(1)} all-to-all(bf16[2,128,4096]{2,1,0:T(8,128)(2,1)S(1)} %pad_maximum_fusion), channel_id=1, replica_groups=mesh['kv'=2,'seq'=128] {'kv'}, dimensions={0} | all-to-all | bytes 4194304 | tf_op jit(solution)/shard_map/all_to_all | solution.py:58
  20.3 3.4 convolution_convert_fusion.1
  25.3 10.9 %collective-permute-done = bf16[2,256,4,128]{3,1,2,0:T(8,128)(2,1)S(1)} collective-permute-done((bf16[2,256,4,128]{3,1,2,0:T(8,128)(2,1)S(1)}, bf16[2,256,4,128]{3,1,2,0:T(8,128)(2,1)S(1)}, u32[]{:S(2)}, u32[]{:S(2)}) %collective-permute-start) | collective-permute-done | bytes 524320 | tf_op jit(solution)/shard_map/ppermute | solution.py:14
  36.1 4.1 %collective-permute-start.1 = (bf16[2,256,4,128]{3,1,2,0:T(8,128)(2,1)S(1)}, bf16[2,256,4,128]{3,1,2,0:T(8,128)(2,1)S(1)}, u32[]{:S(2)}, u32[]{:S(2)}) collective-permute-start(bf16[2,256,4,128]{3,1,2,0:T(8,128)(2,1)S(1)} %collective-permute-done), channel_id=1, source_target_pairs={{0,1},{1,2},{2,3},{3,4},{4,5},{5,6},{6,7},{7,8},{8,9},{9,10},{10,1... | collective-permute-start | bytes 1572872 | tf_op jit(solution)/shard_map/ppermute | solution.py:14
  40.3 10.0 %collective-permute-done.1 = bf16[2,256,4,128]{3,1,2,0:T(8,128)(2,1)S(1)} collective-permute-done((bf16[2,256,4,128]{3,1,2,0:T(8,128)(2,1)S(1)}, bf16[2,256,4,128]{3,1,2,0:T(8,128)(2,1)S(1)}, u32[]{:S(2)}, u32[]{:S(2)}) %collective-permute-start.1) | collective-permute-done | bytes 524320 | tf_op jit(solution)/shard_map/ppermute | solution.py:14
  51.1 4.1 %collective-permute-start.2 = (bf16[2,256,4,128]{3,1,2,0:T(8,128)(2,1)S(1)}, bf16[2,256,4,128]{3,1,2,0:T(8,128)(2,1)S(1)}, u32[]{:S(2)}, u32[]{:S(2)}) collective-permute-start(bf16[2,256,4,128]{3,1,2,0:T(8,128)(2,1)S(1)} %collective-permute-done.1), channel_id=1, source_target_pairs={{0,1},{1,2},{2,3},{3,4},{4,5},{5,6},{6,7},{7,8},{8,9},{9,10},{10,1... | collective-permute-start | bytes 1572872 | tf_op jit(solution)/shard_map/ppermute | solution.py:14
  55.2 9.1 %collective-permute-done.2 = bf16[2,256,4,128]{3,1,2,0:T(8,128)(2,1)S(1)} collective-permute-done((bf16[2,256,4,128]{3,1,2,0:T(8,128)(2,1)S(1)}, bf16[2,256,4,128]{3,1,2,0:T(8,128)(2,1)S(1)}, u32[]{:S(2)}, u32[]{:S(2)}) %collective-permute-start.2) | collective-permute-done | bytes 524320 | tf_op jit(solution)/shard_map/ppermute | solution.py:14
  64.4 4.9 %collective-permute-start.3 = (bf16[2,256,4,128]{3,1,2,0:T(8,128)(2,1)S(1)}, bf16[2,256,4,128]{3,1,2,0:T(8,128)(2,1)}, u32[]{:S(2)}, u32[]{:S(2)}) collective-permute-start(bf16[2,256,4,128]{3,1,2,0:T(8,128)(2,1)S(1)} %collective-permute-done.2), channel_id=1, source_target_pairs={{0,1},{1,2},{2,3},{3,4},{4,5},{5,6},{6,7},{7,8},{8,9},{9,10},{10,1... | collective-permute-start | bytes 1572872 | tf_op jit(solution)/shard_map/ppermute | solution.py:14
  69.3 7.5 %collective-permute-done.3 = bf16[2,256,4,128]{3,1,2,0:T(8,128)(2,1)} collective-permute-done((bf16[2,256,4,128]{3,1,2,0:T(8,128)(2,1)S(1)}, bf16[2,256,4,128]{3,1,2,0:T(8,128)(2,1)}, u32[]{:S(2)}, u32[]{:S(2)}) %collective-permute-start.3) | collective-permute-done | bytes 524320 | tf_op jit(solution)/shard_map/ppermute | solution.py:14
  76.8 5.0 %collective-permute-start.4 = (bf16[2,256,4,128]{3,1,2,0:T(8,128)(2,1)}, bf16[2,256,4,128]{3,1,2,0:T(8,128)(2,1)}, u32[]{:S(2)}, u32[]{:S(2)}) collective-permute-start(bf16[2,256,4,128]{3,1,2,0:T(8,128)(2,1)} %collective-permute-done.3), channel_id=1, source_target_pairs={{0,1},{1,2},{2,3},{3,4},{4,5},{5,6},{6,7},{7,8},{8,9},{9,10},{10,1... | collective-permute-start | bytes 1572872 | tf_op jit(solution)/shard_map/ppermute | solution.py:14
  81.8 9.2 %convolution_convert_fusion = bf16[256,2048]{1,0:T(8,128)(2,1)} fusion(bf16[256,4096]{1,0:T(8,128)(2,1)S(1)} %bitcast.285, bf16[4096,2048]{1,0:T(8,128)(2,1)} %param.12), kind=kOutput, calls=%fused_computation.106 | convolution fusion | flops 4295491584 | bytes 19922944 | tf_op jit(solution)/shard_map/dot_general | solution.py:62
  91.0 5.1 %collective-permute-start.5 = (bf16[2,256,4,128]{3,1,2,0:T(8,128)(2,1)}, bf16[2,256,4,128]{3,1,2,0:T(8,128)(2,1)}, u32[]{:S(2)}, u32[]{:S(2)}) collective-permute-start(bf16[2,256,4,128]{3,1,2,0:T(8,128)(2,1)} %collective-permute-done.4), channel_id=1, source_target_pairs={{0,1},{1,2},{2,3},{3,4},{4,5},{5,6},{6,7},{7,8},{8,9},{9,10},{10,1... | collective-permute-start | bytes 1572872 | tf_op jit(solution)/shard_map/ppermute | solution.py:14
  100.5 2.3 collective-permute-done.5
  102.8 6.2 %collective-permute-start.6 = (bf16[2,256,4,128]{3,1,2,0:T(8,128)(2,1)}, bf16[2,256,4,128]{3,1,2,0:T(8,128)(2,1)S(1)}, u32[]{:S(2)}, u32[]{:S(2)}) collective-permute-start(bf16[2,256,4,128]{3,1,2,0:T(8,128)(2,1)} %collective-permute-done.5), channel_id=1, source_target_pairs={{0,1},{1,2},{2,3},{3,4},{4,5},{5,6},{6,7},{7,8},{8,9},{9,10},{10,1... | collective-permute-start | bytes 1572872 | tf_op jit(solution)/shard_map/ppermute | solution.py:14
  110.3 5.3 %collective-permute-done.6 = bf16[2,256,4,128]{3,1,2,0:T(8,128)(2,1)S(1)} collective-permute-done((bf16[2,256,4,128]{3,1,2,0:T(8,128)(2,1)}, bf16[2,256,4,128]{3,1,2,0:T(8,128)(2,1)S(1)}, u32[]{:S(2)}, u32[]{:S(2)}) %collective-permute-start.6) | collective-permute-done | bytes 524320 | tf_op jit(solution)/shard_map/ppermute | solution.py:14
  115.6 6.5 %collective-permute-start.7 = (bf16[2,256,4,128]{3,1,2,0:T(8,128)(2,1)S(1)}, bf16[2,256,4,128]{3,1,2,0:T(8,128)(2,1)S(1)}, u32[]{:S(2)}, u32[]{:S(2)}) collective-permute-start(bf16[2,256,4,128]{3,1,2,0:T(8,128)(2,1)S(1)} %collective-permute-done.6), channel_id=1, source_target_pairs={{0,1},{1,2},{2,3},{3,4},{4,5},{5,6},{6,7},{7,8},{8,9},{9,10},{10,1... | collective-permute-start | bytes 1572872 | tf_op jit(solution)/shard_map/ppermute | solution.py:14
  124.5 3.6 %collective-permute-done.7 = bf16[2,256,4,128]{3,1,2,0:T(8,128)(2,1)S(1)} collective-permute-done((bf16[2,256,4,128]{3,1,2,0:T(8,128)(2,1)S(1)}, bf16[2,256,4,128]{3,1,2,0:T(8,128)(2,1)S(1)}, u32[]{:S(2)}, u32[]{:S(2)}) %collective-permute-start.7) | collective-permute-done | bytes 524320 | tf_op jit(solution)/shard_map/ppermute | solution.py:14
  129.9 120.6 %while.12 = (s32[]{:T(128)}, bf16[4,256,4,128]{1,3,2,0:T(8,128)(2,1)}, bf16[4,9,256,128]{3,2,1,0:T(8,128)(2,1)S(1)}, bf16[4,9,256,128]{3,2,1,0:T(8,128)(2,1)}, b...) while((s32[]{:T(128)}, ...), condition=%wide.region_12.13_spmd.clone.clone, body=%wide.region_1.12_spmd.clone.clone.sunk | while | flops 1230764032 | bytes 72335304 | solution.py:102
  130.5 2.3 fusion.108
  132.8 2.3 fusion.109
  137.3 2.3 fusion.111
  139.6 2.3 fusion.112
  142.0 2.3 fusion.113
  144.3 2.3 fusion.114
  146.5 2.3 fusion.115
  148.9 2.3 fusion.116
  151.2 5.1 %convert_reduce_fusion.2 = f32[4,256]{1,0:T(4,128)S(1)} fusion(f32[4,256,2304]{1,2,0:T(8,128)} %get-tuple-element.530, f32[4,256]{1,0:T(4,128)S(1)} %maximum_maximum_fusion.2), kind=kLoop, calls=%fused_computation.10.clone.1 | loop fusion | flops 9436160 | bytes 9445376 | tf_op jit(solution)/shard_map/while/body/eval_jaxpr/reduce_sum | solution.py:38
  157.6 2.4 fusion.117
  160.6 2.3 fusion.108
  162.9 2.3 fusion.109
  165.2 2.3 fusion.110
  167.5 2.3 fusion.111
  169.8 2.4 fusion.112
  172.1 2.3 fusion.113
  174.4 2.3 fusion.114
  176.7 2.3 fusion.115
  179.0 2.3 fusion.116
  181.4 5.1 %convert_reduce_fusion.2 = f32[4,256]{1,0:T(4,128)S(1)} fusion(f32[4,256,2304]{1,2,0:T(8,128)} %get-tuple-element.530, f32[4,256]{1,0:T(4,128)S(1)} %maximum_maximum_fusion.2), kind=kLoop, calls=%fused_computation.10.clone.1 | loop fusion | flops 9436160 | bytes 9445376 | tf_op jit(solution)/shard_map/while/body/eval_jaxpr/reduce_sum | solution.py:38
  187.7 2.4 fusion.117
  190.8 2.3 fusion.108
  193.1 2.3 fusion.109
  195.3 2.3 fusion.110
  197.6 2.3 fusion.111
  199.9 2.4 fusion.112
  202.3 2.3 fusion.113
  204.6 2.3 fusion.114
  206.8 2.3 fusion.115
  209.2 2.3 fusion.116
  211.5 5.1 %convert_reduce_fusion.2 = f32[4,256]{1,0:T(4,128)S(1)} fusion(f32[4,256,2304]{1,2,0:T(8,128)} %get-tuple-element.530, f32[4,256]{1,0:T(4,128)S(1)} %maximum_maximum_fusion.2), kind=kLoop, calls=%fused_computation.10.clone.1 | loop fusion | flops 9436160 | bytes 9445376 | tf_op jit(solution)/shard_map/while/body/eval_jaxpr/reduce_sum | solution.py:38
  217.9 2.4 fusion.117
  220.9 2.3 fusion.108
  223.2 2.3 fusion.109
  227.8 2.3 fusion.111
  230.1 2.4 fusion.112
  232.4 2.3 fusion.113
  234.7 2.3 fusion.114
  237.0 2.3 fusion.115
  239.3 2.3 fusion.116
  241.7 5.1 %convert_reduce_fusion.2 = f32[4,256]{1,0:T(4,128)S(1)} fusion(f32[4,256,2304]{1,2,0:T(8,128)} %get-tuple-element.530, f32[4,256]{1,0:T(4,128)S(1)} %maximum_maximum_fusion.2), kind=kLoop, calls=%fused_computation.10.clone.1 | loop fusion | flops 9436160 | bytes 9445376 | tf_op jit(solution)/shard_map/while/body/eval_jaxpr/reduce_sum | solution.py:38
  248.0 2.4 fusion.117
  250.5 12.7 %fusion.86 = f32[256,4096]{1,0:T(8,128)} fusion(bf16[256,2048]{0,1:T(8,128)(2,1)} %bitcast.286, bf16[2048,4096]{1,0:T(8,128)(2,1)} %param.15), kind=kOutput, calls=%fused_computation.143 | convolution fusion | flops 4294967296 | bytes 22020096 | tf_op jit(solution)/shard_map/dot_general | solution.py:111
  264.7 79.6 %all-reduce.2.cloned.1.call-done = f32[256,4096]{1,0:T(8,128)} async-done(((f32[256,4096]{1,0:T(8,128)}), f32[256,4096]{1,0:T(8,128)}) %all-reduce.2.cloned.1.call-update) | async-done | bytes 4194320 | tf_op jit(solution)/shard_map/psum | solution.py:111
  344.3 2.7 dynamic-slice_convert_fusion
  347.0 2.8 fusion.74
  (77 shorter events, 30.3 us)
Async XLA Ops:
  7.2 337.1 %all-reduce.2.cloned.1.call-start = ((), (), s32[]{:S(2)}) async-start(), calls=%async_computation.1 | async-start | bytes 8388608 | tf_op jit(solution)/shard_map/psum | solution.py:111
  8.7 10.2 %copy-start.9 = (bf16[4096,512]{1,0:T(8,128)(2,1)S(1)}, bf16[4096,512]{1,0:T(8,128)(2,1)}, u32[]{:S(2)}) copy-start(bf16[4096,512]{1,0:T(8,128)(2,1)} %param.13) | copy-start | bytes 12582916
  23.8 12.3 %collective-permute-start = (bf16[2,256,4,128]{3,1,2,0:T(8,128)(2,1)S(1)}, bf16[2,256,4,128]{3,1,2,0:T(8,128)(2,1)S(1)}, u32[]{:S(2)}, u32[]{:S(2)}) collective-permute-start(bf16[2,256,4,128]{3,1,2,0:T(8,128)(2,1)S(1)} %copy_dynamic-update-slice_fusion), channel_id=1, source_target_pairs={{0,1},{1,2},{2,3},{3,4},{4,5},{5,6},{6,7},{7,8},{8,9},{9,10},{10,1... | collective-permute-start | bytes 1572872 | tf_op jit(solution)/shard_map/ppermute | solution.py:14
  36.1 28.2 %copy-start.5 = (bf16[2,256,4,128]{3,1,2,0:T(8,128)(2,1)}, bf16[2,256,4,128]{3,1,2,0:T(8,128)(2,1)S(1)}, u32[]{:S(2)}) copy-start(bf16[2,256,4,128]{3,1,2,0:T(8,128)(2,1)S(1)} %collective-permute-done) | copy-start | bytes 1572868
  36.1 14.1 %collective-permute-start.1 = (bf16[2,256,4,128]{3,1,2,0:T(8,128)(2,1)S(1)}, bf16[2,256,4,128]{3,1,2,0:T(8,128)(2,1)S(1)}, u32[]{:S(2)}, u32[]{:S(2)}) collective-permute-start(bf16[2,256,4,128]{3,1,2,0:T(8,128)(2,1)S(1)} %collective-permute-done), channel_id=1, source_target_pairs={{0,1},{1,2},{2,3},{3,4},{4,5},{5,6},{6,7},{7,8},{8,9},{9,10},{10,1... | collective-permute-start | bytes 1572872 | tf_op jit(solution)/shard_map/ppermute | solution.py:14
  50.3 0.8 copy-start.3
  51.1 13.3 %collective-permute-start.2 = (bf16[2,256,4,128]{3,1,2,0:T(8,128)(2,1)S(1)}, bf16[2,256,4,128]{3,1,2,0:T(8,128)(2,1)S(1)}, u32[]{:S(2)}, u32[]{:S(2)}) collective-permute-start(bf16[2,256,4,128]{3,1,2,0:T(8,128)(2,1)S(1)} %collective-permute-done.1), channel_id=1, source_target_pairs={{0,1},{1,2},{2,3},{3,4},{4,5},{5,6},{6,7},{7,8},{8,9},{9,10},{10,1... | collective-permute-start | bytes 1572872 | tf_op jit(solution)/shard_map/ppermute | solution.py:14
  64.4 4.9 %copy-start.7 = (bf16[2,256,4,128]{3,1,2,0:T(8,128)(2,1)}, bf16[2,256,4,128]{3,1,2,0:T(8,128)(2,1)S(1)}, u32[]{:S(2)}) copy-start(bf16[2,256,4,128]{3,1,2,0:T(8,128)(2,1)S(1)} %collective-permute-done.2) | copy-start | bytes 1572868
  64.4 12.4 %collective-permute-start.3 = (bf16[2,256,4,128]{3,1,2,0:T(8,128)(2,1)S(1)}, bf16[2,256,4,128]{3,1,2,0:T(8,128)(2,1)}, u32[]{:S(2)}, u32[]{:S(2)}) collective-permute-start(bf16[2,256,4,128]{3,1,2,0:T(8,128)(2,1)S(1)} %collective-permute-done.2), channel_id=1, source_target_pairs={{0,1},{1,2},{2,3},{3,4},{4,5},{5,6},{6,7},{7,8},{8,9},{9,10},{10,1... | collective-permute-start | bytes 1572872 | tf_op jit(solution)/shard_map/ppermute | solution.py:14
  76.8 14.2 %collective-permute-start.4 = (bf16[2,256,4,128]{3,1,2,0:T(8,128)(2,1)}, bf16[2,256,4,128]{3,1,2,0:T(8,128)(2,1)}, u32[]{:S(2)}, u32[]{:S(2)}) collective-permute-start(bf16[2,256,4,128]{3,1,2,0:T(8,128)(2,1)} %collective-permute-done.3), channel_id=1, source_target_pairs={{0,1},{1,2},{2,3},{3,4},{4,5},{5,6},{6,7},{7,8},{8,9},{9,10},{10,1... | collective-permute-start | bytes 1572872 | tf_op jit(solution)/shard_map/ppermute | solution.py:14
  91.0 9.4 %copy-start.6 = (bf16[2,256,4,128]{3,1,2,0:T(8,128)(2,1)S(1)}, bf16[2,256,4,128]{3,1,2,0:T(8,128)(2,1)}, u32[]{:S(2)}) copy-start(bf16[2,256,4,128]{3,1,2,0:T(8,128)(2,1)} %copy-done.5) | copy-start | bytes 1572868
  91.0 18.0 %copy-start.4 = (bf16[2,256,4,128]{3,1,2,0:T(8,128)(2,1)S(1)}, bf16[2,256,4,128]{3,1,2,0:T(8,128)(2,1)}, u32[]{:S(2)}) copy-start(bf16[2,256,4,128]{3,1,2,0:T(8,128)(2,1)} %copy-done.3) | copy-start | bytes 1572868
  91.0 11.8 %collective-permute-start.5 = (bf16[2,256,4,128]{3,1,2,0:T(8,128)(2,1)}, bf16[2,256,4,128]{3,1,2,0:T(8,128)(2,1)}, u32[]{:S(2)}, u32[]{:S(2)}) collective-permute-start(bf16[2,256,4,128]{3,1,2,0:T(8,128)(2,1)} %collective-permute-done.4), channel_id=1, source_target_pairs={{0,1},{1,2},{2,3},{3,4},{4,5},{5,6},{6,7},{7,8},{8,9},{9,10},{10,1... | collective-permute-start | bytes 1572872 | tf_op jit(solution)/shard_map/ppermute | solution.py:14
  99.1 10.1 %copy-start.8 = (bf16[2,256,4,128]{3,1,2,0:T(8,128)(2,1)S(1)}, bf16[2,256,4,128]{3,1,2,0:T(8,128)(2,1)}, u32[]{:S(2)}) copy-start(bf16[2,256,4,128]{3,1,2,0:T(8,128)(2,1)} %copy-done.7) | copy-start | bytes 1572868
  102.8 12.9 %collective-permute-start.6 = (bf16[2,256,4,128]{3,1,2,0:T(8,128)(2,1)}, bf16[2,256,4,128]{3,1,2,0:T(8,128)(2,1)S(1)}, u32[]{:S(2)}, u32[]{:S(2)}) collective-permute-start(bf16[2,256,4,128]{3,1,2,0:T(8,128)(2,1)} %collective-permute-done.5), channel_id=1, source_target_pairs={{0,1},{1,2},{2,3},{3,4},{4,5},{5,6},{6,7},{7,8},{8,9},{9,10},{10,1... | collective-permute-start | bytes 1572872 | tf_op jit(solution)/shard_map/ppermute | solution.py:14
  115.6 12.4 %collective-permute-start.7 = (bf16[2,256,4,128]{3,1,2,0:T(8,128)(2,1)S(1)}, bf16[2,256,4,128]{3,1,2,0:T(8,128)(2,1)S(1)}, u32[]{:S(2)}, u32[]{:S(2)}) collective-permute-start(bf16[2,256,4,128]{3,1,2,0:T(8,128)(2,1)S(1)} %collective-permute-done.6), channel_id=1, source_target_pairs={{0,1},{1,2},{2,3},{3,4},{4,5},{5,6},{6,7},{7,8},{8,9},{9,10},{10,1... | collective-permute-start | bytes 1572872 | tf_op jit(solution)/shard_map/ppermute | solution.py:14
  151.2 6.4 %copy-start = (f32[4,256,2304]{1,2,0:T(8,128)S(1)}, f32[4,256,2304]{1,2,0:T(8,128)}, u32[]{:S(2)}) copy-start(f32[4,256,2304]{1,2,0:T(8,128)} %get-tuple-element.530) | copy-start | bytes 28311556 | tf_op jit(solution)/shard_map/while
  181.3 6.4 %copy-start = (f32[4,256,2304]{1,2,0:T(8,128)S(1)}, f32[4,256,2304]{1,2,0:T(8,128)}, u32[]{:S(2)}) copy-start(f32[4,256,2304]{1,2,0:T(8,128)} %get-tuple-element.530) | copy-start | bytes 28311556 | tf_op jit(solution)/shard_map/while
  211.5 6.4 %copy-start = (f32[4,256,2304]{1,2,0:T(8,128)S(1)}, f32[4,256,2304]{1,2,0:T(8,128)}, u32[]{:S(2)}) copy-start(f32[4,256,2304]{1,2,0:T(8,128)} %get-tuple-element.530) | copy-start | bytes 28311556 | tf_op jit(solution)/shard_map/while
  241.7 6.4 %copy-start = (f32[4,256,2304]{1,2,0:T(8,128)S(1)}, f32[4,256,2304]{1,2,0:T(8,128)}, u32[]{:S(2)}) copy-start(f32[4,256,2304]{1,2,0:T(8,128)} %get-tuple-element.530) | copy-start | bytes 28311556 | tf_op jit(solution)/shard_map/while
  263.1 0.7 copy-start.10
  263.2 83.8 %copy-start.1 = (bf16[128,4096]{1,0:T(8,128)(2,1)S(1)}, bf16[128,4096]{1,0:T(8,128)(2,1)}, u32[]{:S(2)}) copy-start(bf16[128,4096]{1,0:T(8,128)(2,1)} %param.10) | copy-start | bytes 3145732
  264.6 85.1 %copy-start.2 = (bf16[2,2,4,128,128]{4,3,2,1,0:T(8,128)(2,1)}, bf16[2,2,4,128,128]{4,3,2,1,0:T(8,128)(2,1)S(1)}, u32[]{:S(2)}) copy-start(bf16[2,2,4,128,128]{4,3,2,1,0:T(8,128)(2,1)S(1)} %scatter_fusion) | copy-start | bytes 1572868
Sparse Core Ops, SparseCore 0:
  263.3 80.9 all-reduce.1
